TPU v7x, 128 devices: a whole 4x4x4 slice. The times are simulated.
128 devices in a mesh: user: 16 (over y, z), item: 8 (over x, core).
Axes of the slice: x: 4, y: 4, z: 4, core: 2. Of those that a mesh axis runs over, the one named last changes fastest.
Arguments:
- tile_values: bfloat16 [256, 32, 256, 128], P('user', 'item'), may hold values from -600 to 600
- tile_ids: int32 [256, 32], P('user', 'item'), may hold values from 0 to 2047, as said below
- lengths: int32 [256], P('user'), may hold values from 128 to 256
- user_weights: float32 [256, 256], P('user'), may hold values from 0.5 to 16
- time_factor: float32 [256, 256], replicated, may hold values from -0.25 to 2.25
- item_factor: bfloat16 [262144, 256], P(('item', 'user')), may hold values from -0.2421875 to 0.2421875
Outputs:
- slices: bfloat16 [256, 256, 256], P(('user', 'item'))
- new_time: float32 [256, 256], replicated
- new_items: float32 [262144, 256], P(('item', 'user'))
Inputs may be any that keep to these rules, and one draw needn't show every extreme that they name: `tile_ids`: slot block i of a user (slots i * 4 to (i + 1) * 4 - 1) names tiles i * 256 to (i + 1) * 256 - 1. Within the slots of 16 users of one index of user in one slot block, all tiles differ, and at most 8 of them lie in one group of 16 tiles (group g: tiles i * 256 + g * 16 onward); in every slot block some group holds exactly 8 of them for every index of user.
All inputs are finite; a program needn't handle non-finite values.
Results may differ from a plain program's by a relative error of at most 0.014.
Values may be sent and summed in bfloat16 or wider, within the bound.
A program may use at most 128 MiB of HBM per device.

v0:
```python
import jax
import jax.numpy as jnp
from jax import lax
from jax.sharding import PartitionSpec as P

NS_STEPS = 6
HIGHEST = lax.Precision.HIGHEST
EPSILON = 1e-06


def polar_batch(target):
    norm_scale = jnp.sqrt(jnp.sum(target * target, axis=(1, 2), keepdims=True) + EPSILON)
    iterate = target / norm_scale
    for _ in range(NS_STEPS):
        gram = jnp.einsum("krc,krd->kcd", iterate, iterate, precision=HIGHEST)
        iterate = 1.5 * iterate - 0.5 * jnp.einsum("krc,kcd->krd", iterate, gram, precision=HIGHEST)
    return iterate


def spd_solve(gram_matrix, right_side):
    chol_lower = jnp.linalg.cholesky(gram_matrix)
    return jax.scipy.linalg.cho_solve((chol_lower, True), right_side.T).T


def body(tile_values, tile_ids, lengths, user_weights, time_factor, item_factor):
    user_count = lax.axis_size("user")
    item_count = lax.axis_size("item")
    item_pos = lax.axis_index("item")
    users_here, slots_user, time_rows, tile_width = tile_values.shape
    rank_size = time_factor.shape[0]
    tiles_owned = item_factor.shape[0] // tile_width
    slot_count = users_here * slots_user
    share_count = users_here // item_count
    flat_ids = (tile_ids - item_pos * (tiles_owned * user_count)).reshape(slot_count)
    live = jnp.arange(time_rows, dtype=jnp.int32)[None, :] < lengths[:, None]
    shard_rows = lax.all_gather(item_factor, "user", axis=0, tiled=True)
    panels = shard_rows.reshape(tiles_owned * user_count, tile_width, rank_size)[flat_ids]
    panels = panels.reshape(users_here, slots_user, tile_width, rank_size)
    partial = jnp.einsum("ksrt,kstc->krc", tile_values, panels, preferred_element_type=jnp.float32)
    partial = jnp.where(live[:, :, None], partial, 0.0)
    share_start = item_pos * share_count
    share_weights = lax.dynamic_slice_in_dim(user_weights, share_start, share_count, 0)
    projection = lax.psum_scatter(partial, "item", scatter_dimension=0, tiled=True)
    scaled = projection * share_weights[:, None, :]
    polar = polar_batch(jnp.einsum("krc,dc->krd", scaled, time_factor, precision=HIGHEST))
    slices = polar.astype(jnp.bfloat16)
    time_term = jnp.einsum("krc,krd->cd", polar, scaled, precision=HIGHEST)
    weight_term = jnp.dot(share_weights.T, share_weights, precision=HIGHEST)
    item_term = jnp.dot(item_factor.T, item_factor, preferred_element_type=jnp.float32)
    sums = lax.psum((time_term, weight_term, item_term), "item")
    time_mttkrp, weight_gram, item_inner = lax.psum(sums, "user")
    polar_all = lax.all_gather(slices, "item", axis=0, tiled=True).astype(jnp.float32)
    time_raw = spd_solve(item_inner * weight_gram, time_mttkrp)
    new_time = time_raw / jnp.sqrt(jnp.sum(time_raw * time_raw, axis=0, keepdims=True) + EPSILON)
    item_gram = jnp.dot(new_time.T, new_time, precision=HIGHEST) * weight_gram
    user_maps = (
        jnp.einsum("krc,cd->krd", polar_all, new_time, precision=HIGHEST) * user_weights[:, None, :]
    )
    user_maps = jnp.where(live[:, :, None], user_maps, 0.0).astype(jnp.bfloat16)
    tile_terms = jnp.einsum(
        "ksrt,krc->kstc", tile_values, user_maps, preferred_element_type=jnp.float32
    ).astype(jnp.bfloat16)
    tile_terms = tile_terms.reshape(slot_count, tile_width * rank_size)
    row_count = tiles_owned * tile_width * user_count
    wanted = jnp.arange(row_count // tile_width, dtype=jnp.int32)
    hits = (flat_ids[None, :] == wanted[:, None]).astype(jnp.bfloat16)
    summed = jnp.dot(hits, tile_terms, preferred_element_type=jnp.float32)
    item_mttkrp = lax.psum_scatter(
        summed.reshape(row_count, rank_size).astype(jnp.bfloat16),
        "user",
        scatter_dimension=0,
        tiled=True,
    ).astype(jnp.float32)
    new_items = spd_solve(item_gram, item_mttkrp)
    return (slices, new_time, new_items)


def solution(mesh):
    in_specs = (
        P("user", "item", None, None),
        P("user", "item"),
        P("user"),
        P("user", None),
        P(),
        P(("item", "user"), None),
    )
    out_specs = (P(("user", "item"), None, None), P(), P(("item", "user"), None))
    return jax.shard_map(body, mesh=mesh, in_specs=in_specs, out_specs=out_specs, check_vma=False)
```

profile of v0, /device:TPU:1, one launch (start us, length us, event | category | flops | bytes accessed | tf_op | source)
XLA Modules:
  0.0 606.0 jit_solution(13550863670987385643)
XLA Ops:
  7.2 0.7 all-gather.3.cloned.1.call-update
  8.0 0.7 broadcast_subtract_fusion
  8.9 0.7 iota_compare_fusion.5
  9.6 114.9 %all-gather.3.cloned.1.call-done = bf16[32768,256]{1,0:T(8,128)(2,1)} async-done(((bf16[2048,256]{1,0:T(8,128)(2,1)}), bf16[32768,256]{1,0:T(8,128)(2,1)}) %all-gather.3.cloned.1.call-update) | async-done | bytes 16777232 | tf_op jit(solution)/shard_map/all_gather | solution.py:36
  124.5 8.5 %gather_fusion = bf16[64,128,256]{2,1,0:T(8,128)(2,1)} fusion(bf16[256,128,256]{2,1,0:T(8,128)(2,1)} %bitcast.145, s32[1024]{0:T(1024)S(1)} %pad_clamp_fusion), kind=kCustom, calls=%fused_computation | custom fusion | bytes 8388864 | tf_op jit(solution)/shard_map/gather | solution.py:37
  133.0 6.7 %fusion = f32[16,256,256]{1,2,0:T(8,128)} fusion(bf16[16,4,128,256]{3,2,1,0:T(8,128)(2,1)} %bitcast.142, bf16[16,4,256,128]{3,2,1,0:T(8,128)(2,1)} %param.7, pred[16,256]{1,0:T(8,128)(4,1)S(1)} %iota_compare_fusion.5), kind=kOutput, calls=%fused_computation.7 | convolution fusion | flops 1074790400 | bytes 12587008 | tf_op jit(solution)/shard_map/ksrt,kstc->krc/dot_general | solution.py:39
  139.9 0.6 copy-done.7
  140.5 1.1 fusion.53
  141.7 1.2 fusion.52
  142.9 31.8 %reduce-scatter.3.cloned.1.call-done = f32[2,256,256]{1,2,0:T(8,128)} async-done(((f32[16,256,256]{1,2,0:T(8,128)}), f32[2,256,256]{1,2,0:T(8,128)}) %reduce-scatter.3.cloned.1.call-update) | async-done | bytes 524304 | tf_op jit(solution)/shard_map/reduce_scatter | solution.py:43
  174.7 2.2 multiply_reduce_fusion
  176.9 1.2 fusion.22
  178.1 0.7 fusion.7
  178.8 1.1 fusion.47
  179.9 0.7 fusion.6
  180.5 1.1 fusion.48
  181.6 0.7 fusion.5
  182.3 1.1 fusion.49
  183.4 0.7 fusion.4
  184.1 1.1 fusion.50
  185.1 0.7 fusion.3
  185.8 1.1 fusion.51
  186.9 1.4 fusion.46
  188.3 2.0 convolution_bitcast_fusion
  190.3 61.9 %all-reduce.8.cloned.1.call-done = (f32[256,256]{1,0:T(8,128)}, f32[256,256]{0,1:T(8,128)}, f32[256,256]{0,1:T(8,128)}) async-done(((f32[256,256]{1,0:T(8,128)}, f32[256,256]{0,1:T(8,128)}, f32[256,256]{0,1:T(8,128)}), (f32[256,256]{1,0:T(8,128)}, f32[256,256]{0,1:T(8,128)}, f32[256,256]{0,1:T(8,128)})) %all-reduce.8.cloned.1.call-update) | async-done | bytes 786448 | tf_op jit(solution)/shard_map/psum | solution.py:50
  252.8 89.9 %all-reduce.6.cloned.1.call-done = (f32[256,256]{0,1:T(8,128)}, f32[256,256]{0,1:T(8,128)}, f32[256,256]{0,1:T(8,128)}) async-done(((f32[256,256]{0,1:T(8,128)}, f32[256,256]{0,1:T(8,128)}, f32[256,256]{0,1:T(8,128)}), (f32[256,256]{0,1:T(8,128)}, f32[256,256]{0,1:T(8,128)}, f32[256,256]{0,1:T(8,128)})) %all-reduce.6.cloned.1.call-update) | async-done | bytes 786448 | tf_op jit(solution)/shard_map/psum | solution.py:51
  342.7 1.1 mul.88
  344.0 11.7 %cholesky.130 = f32[128,128]{1,0:T(8,128)S(1)} custom-call(f32[128,128]{1,0:T(8,128)S(1)} %cholesky.194), custom_call_target="Cholesky" | custom-call | tf_op jit(solution)/shard_map/jit(cholesky)/cholesky | solution.py:21
  355.8 9.8 %custom-call.25 = f32[1,128,128]{1,2,0:T(8,128)S(1)} custom-call(f32[1,128,128]{2,1,0:T(8,128)S(1)} %get-tuple-element.62), custom_call_target="InvertDiagBlocksLowerTriangular" | custom-call | tf_op jit(solution)/shard_map/jit(cholesky)/cholesky | solution.py:21
  366.1 11.7 %cholesky.147 = f32[128,128]{1,0:T(8,128)S(1)} custom-call(f32[128,128]{1,0:T(8,128)S(1)} %convolution_subtract_fusion.5), custom_call_target="Cholesky" | custom-call | tf_op jit(solution)/shard_map/jit(cholesky)/cholesky | solution.py:21
  377.9 0.7 compare_reduce_fusion.2
  380.0 4.3 while.2
  380.3 0.6 fusion.101
  380.9 1.4 bitcast_dynamic-update-slice_fusion.4
  382.3 0.6 fusion.101
  382.9 1.4 bitcast_dynamic-update-slice_fusion.4
  384.4 19.7 %custom-call.22 = f32[2,128,128]{1,2,0:T(8,128)S(1)} custom-call(f32[2,128,128]{2,1,0:T(8,128)S(1)} %get-tuple-element.11), custom_call_target="InvertDiagBlocksLowerTriangular" | custom-call | tf_op jit(solution)/shard_map/jit(_cho_solve)/triangular_solve | solution.py:22
  406.1 3.6 select_convert_fusion
  409.8 3.2 convert_bitcast_fusion
  413.0 6.8 %copy.78 = bf16[8,8,128,256]{3,1,2,0:T(8,128)(2,1)} copy(bf16[8,8,128,256]{2,3,1,0:T(8,128)(2,1)} %bitcast.143) | data formatting | bytes 8388608
  419.8 10.2 %convolution_convert_fusion = bf16[256,32768]{1,0:T(8,128)(2,1)} fusion(bf16[64,32768]{1,0:T(8,128)(2,1)} %bitcast.144, s32[64]{0:T(128)S(1)} %eq.15), kind=kOutput, calls=%fused_computation.5 | convolution fusion | flops 1082146816 | bytes 20971776 | tf_op jit(solution)/shard_map/dot_general | solution.py:67
  430.0 25.6 %convert_element_type.26 = bf16[32768,256]{1,0:T(8,128)(2,1)} reshape(bf16[256,32768]{1,0:T(8,128)(2,1)} %convolution_convert_fusion) | data formatting | bytes 33554432 | tf_op jit(solution)/shard_map/convert_element_type | solution.py:69
  455.6 21.6 %copy.58 = bf16[32768,256]{0,1:T(8,128)(2,1)} copy(bf16[32768,256]{1,0:T(8,128)(2,1)} %convert_element_type.26) | data formatting | bytes 33554432 | tf_op jit(solution)/shard_map/convert_element_type | solution.py:69
  477.4 0.8 copy.59
  478.2 0.5 convolution_multiply_fusion.6
  478.9 11.7 %cholesky.164 = f32[128,128]{1,0:T(8,128)S(1)} custom-call(f32[128,128]{1,0:T(8,128)S(1)} %cholesky.197), custom_call_target="Cholesky" | custom-call | tf_op jit(solution)/shard_map/jit(cholesky)/cholesky | solution.py:21
  490.7 9.8 %custom-call.26 = f32[1,128,128]{1,2,0:T(8,128)S(1)} custom-call(f32[1,128,128]{2,1,0:T(8,128)S(1)} %get-tuple-element.58), custom_call_target="InvertDiagBlocksLowerTriangular" | custom-call | tf_op jit(solution)/shard_map/jit(cholesky)/cholesky | solution.py:21
  501.0 11.7 %cholesky.181 = f32[128,128]{1,0:T(8,128)S(1)} custom-call(f32[128,128]{1,0:T(8,128)S(1)} %convolution_subtract_fusion.4), custom_call_target="Cholesky" | custom-call | tf_op jit(solution)/shard_map/jit(cholesky)/cholesky | solution.py:21
  512.7 0.6 compare_reduce_fusion.1
  513.4 0.7 compare_reduce_fusion
  515.4 4.0 while.3
  515.5 0.6 fusion.102
  516.0 1.4 bitcast_dynamic-update-slice_fusion.5
  517.4 0.6 fusion.102
  518.0 1.4 bitcast_dynamic-update-slice_fusion.5
  519.4 19.8 %custom-call.23 = f32[2,128,128]{1,2,0:T(8,128)S(1)} custom-call(f32[2,128,128]{2,1,0:T(8,128)S(1)} %get-tuple-element.19), custom_call_target="InvertDiagBlocksLowerTriangular" | custom-call | tf_op jit(solution)/shard_map/jit(_cho_solve)/triangular_solve | solution.py:22
  539.2 49.8 %reduce-scatter.5.cloned.1.call-done = bf16[2048,256]{0,1:T(8,128)(2,1)} async-done(((bf16[32768,256]{0,1:T(8,128)(2,1)}), bf16[2048,256]{0,1:T(8,128)(2,1)}) %reduce-scatter.5.cloned.1.call-update) | async-done | bytes 1048592 | tf_op jit(solution)/shard_map/reduce_scatter | solution.py:68
  589.1 1.7 fusion.8
  590.7 2.1 convolution_subtract_fusion.1
  592.8 1.1 fusion.35
  593.9 1.0 fusion.34
  594.9 1.0 convolution_subtract_fusion
  595.9 1.0 fusion.33
  597.1 1.8 copy.60
  (70 shorter events, 4.9 us)
Async XLA Ops:
  7.2 167.5 %copy-start = (f32[256,256]{1,0:T(8,128)S(1)}, f32[256,256]{1,0:T(8,128)}, u32[]{:S(2)}) copy-start(f32[256,256]{1,0:T(8,128)} %param.11) | copy-start | bytes 786436
  7.2 117.4 %all-gather.3.cloned.1.call-start = ((), (), s32[]{:S(2)}) async-start(), calls=%async_computation.2 | async-start | bytes 17825792 | tf_op jit(solution)/shard_map/all_gather | solution.py:36
  7.9 166.8 %reduce-scatter.3.cloned.1.call-start = ((), (), s32[]{:S(2)}) async-start(), calls=%async_computation.3 | async-start | bytes 4718592 | tf_op jit(solution)/shard_map/reduce_scatter | solution.py:43
  139.8 0.7 copy-start.7
  139.8 1.9 copy-start.4
  139.8 112.4 %all-reduce.8.cloned.1.call-start = ((), (), s32[]{:S(2)}) async-start(), calls=%async_computation.7 | async-start | bytes 1572864 | tf_op jit(solution)/shard_map/psum | solution.py:50
  183.4 4.9 copy-start.3
  190.3 152.5 %all-reduce.6.cloned.1.call-start = ((), (), s32[]{:S(2)}) async-start(), calls=%async_computation.6 | async-start | bytes 1572864 | tf_op jit(solution)/shard_map/psum | solution.py:51
  252.2 153.9 %all-gather.5.cloned.1.call-start = ((), (), s32[]{:S(2)}) async-start(), calls=%async_computation.4 | async-start | bytes 2359296 | tf_op jit(solution)/shard_map/all_gather | solution.py:52
  252.8 336.3 %reduce-scatter.5.cloned.1.call-start = ((), (), s32[]{:S(2)}) async-start(), calls=%async_computation.5 | async-start | bytes 17825792 | tf_op jit(solution)/shard_map/reduce_scatter | solution.py:68
  342.7 61.3 %copy-start.6 = (f32[256,256]{0,1:T(8,128)S(1)}, f32[256,256]{0,1:T(8,128)}, u32[]{:S(2)}) copy-start(f32[256,256]{0,1:T(8,128)} %get-tuple-element.45) | copy-start | bytes 786436
  406.1 3.7 copy-start.2
  477.3 1.0 copy-start.5
  595.9 3.0 copy-start.1
Sparse Core Ops, SparseCore 0:
  10.1 114.3 all-gather.2
  139.9 34.6 reduce-scatter.2
  190.4 61.7 all-reduce.7
  255.6 87.0 all-reduce.5
  344.9 26.7 all-gather.4
  477.4 111.6 reduce-scatter.4
where the time goes:
time: 618 us; the launch traced here: 606 us
  waiting for transfers between devices  350 us (57%)
  other arithmetic  111 us (18%)
  local copies, waits for them, and re-layouts  74.5 us (12%)
  matrix products  52.8 us (9%)
  between operations  17.4 us (3%)
    all_gather x1, waiting for transfers between devices, body(): shard_rows = lax.all_gather(item_factor, 'user', axis=0, tiled=True)  115 us
    psum x1, waiting for transfers between devices, body(): time_mttkrp, weight_gram, item_inner = lax.psum(sums, 'user')  89.9 us
    another operation x13, other arithmetic, spd_solve(): chol_lower = jnp.linalg.cholesky(gram_matrix)  68.7 us
    psum x1, waiting for transfers between devices, body(): sums = lax.psum((time_term, weight_term, item_term), 'item')  61.9 us
    reduce_scatter x1, waiting for transfers between devices, body(): lax.psum_scatter(summed.reshape(row_count, rank_size).astype(jnp.bfloat16...  49.8 us
    convert_element_type x2, local copies, waits for them, and re-layouts, body(): summed.reshape(row_count, rank_size).astype(jnp.bfloat16)  47.3 us
    another operation x5, other arithmetic, spd_solve(): return jax.scipy.linalg.cho_solve((chol_lower, True), right_side.T).T  39.6 us
    reduce_scatter x1, waiting for transfers between devices, body(): lax.psum_scatter(partial, 'item', scatter_dimension=0, tiled=True)  31.8 us
  transfers between devices with their start and end apart: 6, of which 5 were waited for; matrix products, arithmetic and copies ran while one was open for 21% of the time, Pallas kernels for 0%

commit v1 on v0

--- a/solution.py
+++ b/solution.py
@@ -33,7 +33,8 @@
     share_count = users_here // item_count
     flat_ids = (tile_ids - item_pos * (tiles_owned * user_count)).reshape(slot_count)
     live = jnp.arange(time_rows, dtype=jnp.int32)[None, :] < lengths[:, None]
-    shard_rows = lax.all_gather(item_factor, "user", axis=0, tiled=True)
+    stack = jnp.stack([item_factor] * lax.axis_size("user"))
+    shard_rows = jnp.concatenate(lax.all_to_all(stack, "user", 0, 0), axis=0)
     panels = shard_rows.reshape(tiles_owned * user_count, tile_width, rank_size)[flat_ids]
     panels = panels.reshape(users_here, slots_user, tile_width, rank_size)
     partial = jnp.einsum("ksrt,kstc->krc", tile_values, panels, preferred_element_type=jnp.float32)

time: 618 us -> 807 us (1.31); the launches traced: 606 us -> 803 us
  waiting for transfers between devices: 350 us -> 533 us
  starting transfers between devices: 0.24 us -> 9.5 us
    all_to_all x0 -> x1, waiting for transfers between devices: none -> 293 us  [body(): shard_rows = jnp.concatenate(lax.all_to_all(stack, 'user', 0, 0), axis=0)]
    all_gather x1 -> x0, waiting for transfers between devices: 115 us -> none  [body(): shard_rows = lax.all_gather(item_factor, 'user', axis=0, tiled=True)]
    all_to_all x0 -> x1, starting transfers between devices: none -> 8.77 us  [body(): shard_rows = jnp.concatenate(lax.all_to_all(stack, 'user', 0, 0), axis=0)]
  transfers between devices with their start and end apart: 6 -> 6, of which waited for: 5 -> 5; matrix products, arithmetic and copies ran while one was open for 21% -> 15% of each run, Pallas kernels for 0% -> 0%
where the time goes in v1:
time: 807 us; the launch traced here: 803 us
  waiting for transfers between devices  533 us (66%)
  other arithmetic  110 us (14%)
  local copies, waits for them, and re-layouts  80.6 us (10%)
  matrix products  52.8 us (7%)
  between operations  17 us (2%)
  starting transfers between devices  9.5 us (1%)
    all_to_all x1, waiting for transfers between devices, body(): shard_rows = jnp.concatenate(lax.all_to_all(stack, 'user', 0, 0), axis=0)  293 us
    psum x1, waiting for transfers between devices, body(): time_mttkrp, weight_gram, item_inner = lax.psum(sums, 'user')  90 us
    another operation x13, other arithmetic, spd_solve(): chol_lower = jnp.linalg.cholesky(gram_matrix)  68.6 us
    psum x1, waiting for transfers between devices, body(): sums = lax.psum((time_term, weight_term, item_term), 'item')  61.7 us
    reduce_scatter x1, waiting for transfers between devices, body(): lax.psum_scatter(summed.reshape(row_count, rank_size).astype(jnp.bfloat16...  50 us
    convert_element_type x2, local copies, waits for them, and re-layouts, body(): summed.reshape(row_count, rank_size).astype(jnp.bfloat16)  47.3 us
    another operation x5, other arithmetic, spd_solve(): return jax.scipy.linalg.cho_solve((chol_lower, True), right_side.T).T  39.6 us
    reduce_scatter x1, waiting for transfers between devices, body(): lax.psum_scatter(partial, 'item', scatter_dimension=0, tiled=True)  37.9 us
  transfers between devices with their start and end apart: 6, of which 5 were waited for; matrix products, arithmetic and copies ran while one was open for 15% of the time, Pallas kernels for 0%

profile of v1, /device:TPU:1, one launch (start us, length us, event | category | flops | bytes accessed | tf_op | source)
XLA Modules:
  0.0 803.1 jit_solution(8077666156026588031)
XLA Ops:
  7.2 6.9 stack.2
  14.0 8.8 %all-to-all-start = ((bf16[16,2048,256]{2,1,0:T(8,128)(2,1)}), bf16[16,2048,256]{2,1,0:T(8,128)(2,1)}, u32[]{:S(2)}, u32[]{:S(2)}) async-start(bf16[16,2048,256]{2,1,0:T(8,128)(2,1)} %stack.2), calls=%async_computation | async-start | bytes 33554432 | tf_op jit(solution)/shard_map/all_to_all | solution.py:37
  23.2 293.0 %all-to-all-done = bf16[16,2048,256]{2,1,0:T(8,128)(2,1)} async-done(((bf16[16,2048,256]{2,1,0:T(8,128)(2,1)}), bf16[16,2048,256]{2,1,0:T(8,128)(2,1)}, u32[]{:S(2)}, u32[]{:S(2)}) %all-to-all-start) | async-done | bytes 16777248 | tf_op jit(solution)/shard_map/all_to_all | solution.py:37
  316.1 8.5 %gather_fusion = bf16[64,128,256]{2,1,0:T(8,128)(2,1)} fusion(bf16[256,128,256]{2,1,0:T(8,128)(2,1)} %bitcast, s32[1024]{0:T(1024)S(1)} %pad_clamp_fusion), kind=kCustom, calls=%fused_computation | custom fusion | bytes 8388864 | tf_op jit(solution)/shard_map/gather | solution.py:38
  324.7 6.7 fusion
  331.4 0.6 all-reduce.8.cloned.1.call-start
  332.1 1.1 fusion.53
  333.3 1.2 fusion.52
  334.5 37.9 %reduce-scatter.3.cloned.1.call-done = f32[2,256,256]{1,2,0:T(8,128)} async-done(((f32[16,256,256]{1,2,0:T(8,128)}), f32[2,256,256]{1,2,0:T(8,128)}) %reduce-scatter.3.cloned.1.call-update) | async-done | bytes 524304 | tf_op jit(solution)/shard_map/reduce_scatter | solution.py:44
  372.4 2.2 multiply_reduce_fusion
  374.6 1.2 fusion.22
  375.8 0.7 fusion.7
  376.5 1.1 fusion.47
  377.6 0.7 fusion.6
  378.3 1.1 fusion.48
  379.3 0.7 fusion.5
  380.0 1.1 fusion.49
  381.1 0.7 fusion.4
  381.8 1.1 fusion.50
  382.9 0.7 fusion.3
  383.6 1.1 fusion.51
  384.6 1.4 fusion.46
  386.0 2.0 convolution_bitcast_fusion
  388.0 61.7 %all-reduce.8.cloned.1.call-done = (f32[256,256]{1,0:T(8,128)}, f32[256,256]{0,1:T(8,128)}, f32[256,256]{0,1:T(8,128)}) async-done(((f32[256,256]{1,0:T(8,128)}, f32[256,256]{0,1:T(8,128)}, f32[256,256]{0,1:T(8,128)}), (f32[256,256]{1,0:T(8,128)}, f32[256,256]{0,1:T(8,128)}, f32[256,256]{0,1:T(8,128)})) %all-reduce.8.cloned.1.call-update) | async-done | bytes 786448 | tf_op jit(solution)/shard_map/psum | solution.py:51
  450.0 0.4 all-gather.2.cloned.1.call-update
  450.4 90.0 %all-reduce.6.cloned.1.call-done = (f32[256,256]{0,1:T(8,128)}, f32[256,256]{0,1:T(8,128)}, f32[256,256]{0,1:T(8,128)}) async-done(((f32[256,256]{0,1:T(8,128)}, f32[256,256]{0,1:T(8,128)}, f32[256,256]{0,1:T(8,128)}), (f32[256,256]{0,1:T(8,128)}, f32[256,256]{0,1:T(8,128)}, f32[256,256]{0,1:T(8,128)})) %all-reduce.6.cloned.1.call-update) | async-done | bytes 786448 | tf_op jit(solution)/shard_map/psum | solution.py:52
  540.5 1.1 mul.88
  541.8 11.7 %cholesky.130 = f32[128,128]{1,0:T(8,128)S(1)} custom-call(f32[128,128]{1,0:T(8,128)S(1)} %cholesky.194), custom_call_target="Cholesky" | custom-call | tf_op jit(solution)/shard_map/jit(cholesky)/cholesky | solution.py:21
  553.5 9.8 %custom-call.25 = f32[1,128,128]{1,2,0:T(8,128)S(1)} custom-call(f32[1,128,128]{2,1,0:T(8,128)S(1)} %get-tuple-element.62), custom_call_target="InvertDiagBlocksLowerTriangular" | custom-call | tf_op jit(solution)/shard_map/jit(cholesky)/cholesky | solution.py:21
  563.9 11.7 %cholesky.147 = f32[128,128]{1,0:T(8,128)S(1)} custom-call(f32[128,128]{1,0:T(8,128)S(1)} %convolution_subtract_fusion.5), custom_call_target="Cholesky" | custom-call | tf_op jit(solution)/shard_map/jit(cholesky)/cholesky | solution.py:21
  575.6 0.6 compare_reduce_fusion.2
  577.6 4.0 while.2
  577.8 0.6 fusion.101
  578.4 1.3 bitcast_dynamic-update-slice_fusion.4
  579.7 0.6 fusion.101
  580.3 1.3 bitcast_dynamic-update-slice_fusion.4
  581.6 19.7 %custom-call.22 = f32[2,128,128]{1,2,0:T(8,128)S(1)} custom-call(f32[2,128,128]{2,1,0:T(8,128)S(1)} %get-tuple-element.11), custom_call_target="InvertDiagBlocksLowerTriangular" | custom-call | tf_op jit(solution)/shard_map/jit(_cho_solve)/triangular_solve | solution.py:22
  603.4 3.6 select_convert_fusion
  607.0 3.2 convert_bitcast_fusion
  610.3 6.8 copy.78
  617.1 10.2 %convolution_convert_fusion = bf16[256,32768]{1,0:T(8,128)(2,1)} fusion(bf16[64,32768]{1,0:T(8,128)(2,1)} %bitcast.143, s32[64]{0:T(128)S(1)} %eq.15), kind=kOutput, calls=%fused_computation.5 | convolution fusion | flops 1082146816 | bytes 20971776 | tf_op jit(solution)/shard_map/dot_general | solution.py:68
  627.3 25.6 %convert_element_type.26 = bf16[32768,256]{1,0:T(8,128)(2,1)} reshape(bf16[256,32768]{1,0:T(8,128)(2,1)} %convolution_convert_fusion) | data formatting | bytes 33554432 | tf_op jit(solution)/shard_map/convert_element_type | solution.py:70
  652.9 21.7 %copy.57 = bf16[32768,256]{0,1:T(8,128)(2,1)} copy(bf16[32768,256]{1,0:T(8,128)(2,1)} %convert_element_type.26) | data formatting | bytes 33554432 | tf_op jit(solution)/shard_map/convert_element_type | solution.py:70
  674.8 0.8 copy.58
  675.6 0.5 convolution_multiply_fusion.6
  676.3 11.7 %cholesky.164 = f32[128,128]{1,0:T(8,128)S(1)} custom-call(f32[128,128]{1,0:T(8,128)S(1)} %cholesky.197), custom_call_target="Cholesky" | custom-call | tf_op jit(solution)/shard_map/jit(cholesky)/cholesky | solution.py:21
  688.0 9.8 %custom-call.26 = f32[1,128,128]{1,2,0:T(8,128)S(1)} custom-call(f32[1,128,128]{2,1,0:T(8,128)S(1)} %get-tuple-element.58), custom_call_target="InvertDiagBlocksLowerTriangular" | custom-call | tf_op jit(solution)/shard_map/jit(cholesky)/cholesky | solution.py:21
  698.4 11.7 %cholesky.181 = f32[128,128]{1,0:T(8,128)S(1)} custom-call(f32[128,128]{1,0:T(8,128)S(1)} %convolution_subtract_fusion.4), custom_call_target="Cholesky" | custom-call | tf_op jit(solution)/shard_map/jit(cholesky)/cholesky | solution.py:21
  710.1 0.6 compare_reduce_fusion.1
  710.7 0.7 compare_reduce_fusion
  712.7 4.0 while.3
  712.8 0.6 fusion.102
  713.4 1.4 bitcast_dynamic-update-slice_fusion.5
  714.8 0.6 fusion.102
  715.4 1.4 bitcast_dynamic-update-slice_fusion.5
  716.7 19.8 %custom-call.23 = f32[2,128,128]{1,2,0:T(8,128)S(1)} custom-call(f32[2,128,128]{2,1,0:T(8,128)S(1)} %get-tuple-element.19), custom_call_target="InvertDiagBlocksLowerTriangular" | custom-call | tf_op jit(solution)/shard_map/jit(_cho_solve)/triangular_solve | solution.py:22
  736.6 50.0 %reduce-scatter.5.cloned.1.call-done = bf16[2048,256]{0,1:T(8,128)(2,1)} async-done(((bf16[32768,256]{0,1:T(8,128)(2,1)}), bf16[2048,256]{0,1:T(8,128)(2,1)}) %reduce-scatter.5.cloned.1.call-update) | async-done | bytes 1048592 | tf_op jit(solution)/shard_map/reduce_scatter | solution.py:69
  786.5 1.7 fusion.8
  788.2 2.1 convolution_subtract_fusion.1
  790.3 1.0 fusion.35
  791.3 1.0 fusion.34
  792.4 1.0 convolution_subtract_fusion
  793.4 1.0 fusion.33
  794.6 1.8 copy.59
  (74 shorter events, 4.6 us)
Async XLA Ops:
  7.2 365.3 %copy-start = (f32[256,256]{1,0:T(8,128)S(1)}, f32[256,256]{1,0:T(8,128)}, u32[]{:S(2)}) copy-start(f32[256,256]{1,0:T(8,128)} %param.11) | copy-start | bytes 786436
  14.0 8.8 %copy-start.7 = (s32[16,4]{0,1:T(4,128)S(1)}, s32[16,4]{0,1:T(4,128)}, u32[]{:S(2)}) copy-start(s32[16,4]{0,1:T(4,128)} %param.8) | copy-start | bytes 772
  14.0 9.1 %copy-start.8 = (s32[16]{0:T(128)S(1)}, s32[16]{0:T(128)}, u32[]{:S(2)}) copy-start(s32[16]{0:T(128)} %param.9) | copy-start | bytes 196
  14.0 302.1 %all-to-all-start = ((bf16[16,2048,256]{2,1,0:T(8,128)(2,1)}), bf16[16,2048,256]{2,1,0:T(8,128)(2,1)}, u32[]{:S(2)}, u32[]{:S(2)}) async-start(bf16[16,2048,256]{2,1,0:T(8,128)(2,1)} %stack.2), calls=%async_computation | async-start | bytes 33554432 | tf_op jit(solution)/shard_map/all_to_all | solution.py:37
  22.8 349.6 %reduce-scatter.3.cloned.1.call-start = ((), (), s32[]{:S(2)}) async-start(), calls=%async_computation.3 | async-start | bytes 4718592 | tf_op jit(solution)/shard_map/reduce_scatter | solution.py:44
  331.4 0.7 copy-start.9
  331.4 1.9 copy-start.4
  331.4 118.4 %all-reduce.8.cloned.1.call-start = ((), (), s32[]{:S(2)}) async-start(), calls=%async_computation.7 | async-start | bytes 1572864 | tf_op jit(solution)/shard_map/psum | solution.py:51
  381.1 4.9 copy-start.3
  388.0 152.5 %all-reduce.6.cloned.1.call-start = ((), (), s32[]{:S(2)}) async-start(), calls=%async_computation.6 | async-start | bytes 1572864 | tf_op jit(solution)/shard_map/psum | solution.py:52
  449.8 153.6 %all-gather.2.cloned.1.call-start = ((), (), s32[]{:S(2)}) async-start(), calls=%async_computation.4 | async-start | bytes 2359296 | tf_op jit(solution)/shard_map/all_gather | solution.py:53
  450.4 336.2 %reduce-scatter.5.cloned.1.call-start = ((), (), s32[]{:S(2)}) async-start(), calls=%async_computation.5 | async-start | bytes 17825792 | tf_op jit(solution)/shard_map/reduce_scatter | solution.py:69
  540.5 60.8 %copy-start.6 = (f32[256,256]{0,1:T(8,128)S(1)}, f32[256,256]{0,1:T(8,128)}, u32[]{:S(2)}) copy-start(f32[256,256]{0,1:T(8,128)} %get-tuple-element.45) | copy-start | bytes 786436
  603.4 3.7 copy-start.2
  674.6 1.0 copy-start.5
  793.4 3.0 copy-start.1
Sparse Core Ops, SparseCore 0:
  331.6 40.8 reduce-scatter.2
  388.1 61.6 all-reduce.7
  453.4 87.0 all-reduce.5
  542.6 26.8 all-gather.1
  674.8 111.7 reduce-scatter.4
